TPU v7x, 256 devices: a whole 4x4x8 slice. The times are simulated.
256 devices in a mesh: chan: 8 (over z), tm: 32 (over y, x, core).
Axes of the slice: x: 4, y: 4, z: 8, core: 2. Of those that a mesh axis runs over, the one named last changes fastest.
Arguments:
- symbols: int32 [64, 262144], P('chan', 'tm'), may hold values from 0 to 63
- incidence: int32 [256, 6], P('chan'), may hold values from 0 to 63, as said below
- delays: int32 [256, 6], P('chan'), may hold values from 0 to 63
- gains: float32 [2, 256, 6], P(None, 'chan'), may hold values from -4 to 4
- echoes: bfloat16 [2, 256, 262144], P(None, 'chan', 'tm'), may hold values from -6 to 6
Outputs:
- cancelled: bfloat16 [2, 256, 262144], P(None, 'chan', 'tm')
- weights: float32 [2, 256, 384], P(None, 'chan')
Inputs may be any that keep to these rules, and one draw needn't show every extreme that they name: `incidence`: row r names 6 distinct illuminators, all owned by chan index c = r // 32 or the next index c + 1 taken cyclically: ids from c * 8 to (c + 2) * 8 - 1, modulo 64.
All inputs are finite; a program needn't handle non-finite values.
Results may differ from a plain program's by a relative error of at most 0.024.
Values may be sent and summed in bfloat16 or wider, within the bound.
No kernel may reach another device: no remote copies, remote signals or barrier semaphores. Data moves between devices by JAX's collectives and lax.ppermute only.
A program may use at most 64 MiB of HBM per device.

v0:
```python
import math
import jax
import jax.numpy as jnp
from jax import lax
from jax.sharding import PartitionSpec as P

ACTIVE = 6817
DELAYS = 64
PER_RECV = 6
loading = 0.1
batch_rows = 8
HIGHEST = lax.Precision.HIGHEST


def passed_along(array, axis, by):
    peers = lax.axis_size(axis)
    return lax.ppermute(array, axis, [(i, (i + by) % peers) for i in range(peers)])


def from_behind(block, axis, distance):
    devices = range(lax.axis_size(axis))
    route = [(i - distance, i) for i in devices if i - distance in devices]
    return lax.ppermute(block, axis, route)


def rotation_angle_grid(row_count, col_count, period):
    product = (
        jnp.arange(row_count, dtype=jnp.int32)[:, None]
        * jnp.arange(col_count, dtype=jnp.int32)[None, :]
    )
    phases = (product % period).astype(jnp.float32) * (2.0 * math.pi / period)
    return (jnp.cos(phases), jnp.sin(phases))


def complex_multiply_result(pattern, left_pair, right_pair):
    real_part = jnp.einsum(pattern, left_pair[0], right_pair[0], precision=HIGHEST) - jnp.einsum(
        pattern, left_pair[1], right_pair[1], precision=HIGHEST
    )
    imag_part = jnp.einsum(pattern, left_pair[0], right_pair[1], precision=HIGHEST) + jnp.einsum(
        pattern, left_pair[1], right_pair[0], precision=HIGHEST
    )
    return (real_part, imag_part)


def remodulate(symbols):
    emitter_number, length = symbols.shape
    column_entries = 128
    increment_spacing = length // column_entries
    inphase_amplitude = (2 * (symbols % 8) - 7).astype(jnp.float32) / math.sqrt(42.0)
    quadrature_amplitude = (2 * (symbols // 8) - 7).astype(jnp.float32) / math.sqrt(42.0)
    subcarrier = jnp.arange(length, dtype=jnp.int32) - length // 2
    occupied_tones = (jnp.abs(subcarrier) <= (ACTIVE - 1) // 2).astype(jnp.float32)
    tone_symbols = (
        (inphase_amplitude * occupied_tones).reshape(
            emitter_number, increment_spacing, column_entries
        ),
        (quadrature_amplitude * occupied_tones).reshape(
            emitter_number, increment_spacing, column_entries
        ),
    )
    partial_result = complex_multiply_result(
        "mb,nbd->nmd",
        rotation_angle_grid(increment_spacing, increment_spacing, increment_spacing),
        tone_symbols,
    )
    twiddle = rotation_angle_grid(increment_spacing, column_entries, length)
    partial_result = (
        partial_result[0] * twiddle[0] - partial_result[1] * twiddle[1],
        partial_result[0] * twiddle[1] + partial_result[1] * twiddle[0],
    )
    frequency_spectrum = complex_multiply_result(
        "pho,oj->phj",
        partial_result,
        rotation_angle_grid(column_entries, column_entries, column_entries),
    )
    alternate = (1 - 2 * (jnp.arange(length, dtype=jnp.int32) % 2)).astype(jnp.float32) / math.sqrt(
        ACTIVE
    )
    real_part = (
        jnp.swapaxes(frequency_spectrum[0], 1, 2).reshape(emitter_number, length) * alternate
    )
    imag_part = (
        jnp.swapaxes(frequency_spectrum[1], 1, 2).reshape(emitter_number, length) * alternate
    )
    return jnp.stack([real_part, imag_part], axis=1).astype(jnp.bfloat16)


def lag_table(lag_count):
    spread = jnp.arange(2 * lag_count, dtype=jnp.int32)[:, None, None]
    column = jnp.arange(lag_count, dtype=jnp.int32)[None, :, None]
    lag_pos = jnp.arange(lag_count, dtype=jnp.int32)[None, None, :]
    return (spread == lag_count + column - lag_pos).astype(jnp.float32)


def lag_sums(outer):
    leading = outer.shape[:-2]
    lag_count = outer.shape[-2]
    width = outer.shape[-1]
    flat = outer.reshape(leading + (lag_count * width,))
    flat = jnp.pad(flat, [(0, 0)] * len(leading) + [(0, lag_count)])
    skewed = flat.reshape(leading + (lag_count, width + 1))[..., 1 : lag_count + 1]
    return jnp.flip(jnp.sum(skewed, axis=-2), axis=-1)


def toeplitz_tables(lag_count):
    row_pos = jnp.arange(lag_count, dtype=jnp.int32)[:, None, None]
    col_pos = jnp.arange(lag_count, dtype=jnp.int32)[None, :, None]
    lag_pos = jnp.arange(lag_count, dtype=jnp.int32)[None, None, :]
    lower_part = (row_pos - col_pos == lag_pos).astype(jnp.float32)
    upper_part = ((col_pos - row_pos == lag_pos) & (lag_pos > 0)).astype(jnp.float32)
    return (lower_part, upper_part)


def banded_apply(looked, banded):
    real_part = jnp.einsum(
        "bkqv,bkvp->bqp", looked[:, :, 0], banded[0], preferred_element_type=jnp.float32
    ) - jnp.einsum("bkqv,bkvp->bqp", looked[:, :, 1], banded[1], preferred_element_type=jnp.float32)
    imag_part = jnp.einsum(
        "bkqv,bkvp->bqp", looked[:, :, 0], banded[1], preferred_element_type=jnp.float32
    ) + jnp.einsum("bkqv,bkvp->bqp", looked[:, :, 1], banded[0], preferred_element_type=jnp.float32)
    return (real_part, imag_part)


def local(symbols, incidence, delays, gains, echoes):
    local_refs = remodulate(symbols)
    owned = local_refs.shape[0]
    length = local_refs.shape[2]
    lag_count = DELAYS
    taps_count = PER_RECV * DELAYS
    chan_count = lax.axis_size("chan")
    chan_index = lax.axis_index("chan")
    window_count = 2 * owned
    following = passed_along(local_refs, "chan", -1)
    window = jnp.concatenate([local_refs, following], axis=0)
    previous = from_behind(window[:, :, length - lag_count :], "tm", 1)
    extended = jnp.concatenate([previous, window], axis=2)
    block_count = length // lag_count
    pieces = extended.reshape(window_count, 2, block_count + 1, lag_count)
    frames = jnp.concatenate([pieces[:, :, :-1], pieces[:, :, 1:]], axis=3)
    current = pieces[:, :, 1:]
    tm_count = lax.axis_size("tm")
    tm_index = lax.axis_index("tm")
    scale = 1.0 / (length * tm_count)
    diagonal_table = lag_table(lag_count)
    lag_range = jnp.arange(lag_count, dtype=jnp.int32)

    def pair_row(frame):
        real_part = jnp.einsum(
            "qv,jqp->jpv", frame[0], current[:, 0], preferred_element_type=jnp.float32
        ) + jnp.einsum("qv,jqp->jpv", frame[1], current[:, 1], preferred_element_type=jnp.float32)
        imag_part = jnp.einsum(
            "qv,jqp->jpv", frame[0], current[:, 1], preferred_element_type=jnp.float32
        ) - jnp.einsum("qv,jqp->jpv", frame[1], current[:, 0], preferred_element_type=jnp.float32)
        return jnp.concatenate([lag_sums(real_part), lag_sums(imag_part)], axis=1)

    corr_part = lax.map(pair_row, frames) * scale
    owner_chan = incidence // owned
    slot = (owner_chan - chan_index) % chan_count * owned + incidence % owned
    recv_count = echoes.shape[1]
    group_count = recv_count // batch_rows

    def first_pass(step, carry):
        received_all, cross_all = carry
        start = step * batch_rows
        slots = lax.dynamic_slice_in_dim(slot, start, batch_rows, 0).reshape(-1)
        lag_values = lax.dynamic_slice_in_dim(delays, start, batch_rows, 0)
        gain = lax.dynamic_slice_in_dim(gains, start, batch_rows, 1)
        echo = lax.dynamic_slice_in_dim(echoes, start, batch_rows, 1)
        looked = jnp.take(frames, slots, axis=0).reshape(
            batch_rows, PER_RECV, 2, block_count, 2 * lag_count
        )
        onehot = (lag_values[:, :, None] == lag_range[None, None, :]).astype(jnp.float32)
        gain_taps = gain[:, :, :, None] * onehot[None]
        band = jnp.einsum("vpa,xbka->xbkvp", diagonal_table, gain_taps, precision=HIGHEST)
        band_high = band.astype(jnp.bfloat16)
        band_low = (band - band_high.astype(jnp.float32)).astype(jnp.bfloat16)
        high_re, high_im = banded_apply(looked, band_high)
        low_re, low_im = banded_apply(looked, band_low)
        direct_re = (high_re + low_re).reshape(batch_rows, length)
        direct_im = (high_im + low_im).reshape(batch_rows, length)
        received = jnp.stack(
            [echo[0].astype(jnp.float32) + direct_re, echo[1].astype(jnp.float32) + direct_im]
        ).astype(jnp.bfloat16)
        signal = received.reshape(2, batch_rows, block_count, lag_count)
        real_part = jnp.einsum(
            "bkqv,bqp->bkpv", looked[:, :, 0], signal[0], preferred_element_type=jnp.float32
        ) + jnp.einsum(
            "bkqv,bqp->bkpv", looked[:, :, 1], signal[1], preferred_element_type=jnp.float32
        )
        imag_part = jnp.einsum(
            "bkqv,bqp->bkpv", looked[:, :, 0], signal[1], preferred_element_type=jnp.float32
        ) - jnp.einsum(
            "bkqv,bqp->bkpv", looked[:, :, 1], signal[0], preferred_element_type=jnp.float32
        )
        cross_re = lag_sums(real_part).reshape(batch_rows, taps_count)
        cross_im = lag_sums(imag_part).reshape(batch_rows, taps_count)
        cross_piece = jnp.stack([cross_re, cross_im]) * scale
        received_all = lax.dynamic_update_slice_in_dim(received_all, received, start, 1)
        cross_all = lax.dynamic_update_slice_in_dim(cross_all, cross_piece, start, 1)
        return (received_all, cross_all)

    received_init = jnp.zeros((2, recv_count, length), jnp.bfloat16)
    cross_init = jnp.zeros((2, recv_count, taps_count), jnp.float32)
    received_all, cross_all = lax.fori_loop(0, group_count, first_pass, (received_init, cross_init))
    share = recv_count // tm_count
    corr = lax.psum(corr_part, "tm")
    cross = lax.psum_scatter(cross_all, "tm", scatter_dimension=1, tiled=True)
    mine = lax.dynamic_slice_in_dim(slot, tm_index * share, share, 0)
    selector = (
        mine[:, :, None] == jnp.arange(window_count, dtype=jnp.int32)[None, None, :]
    ).astype(jnp.float32)
    gathered = jnp.einsum("rkw,wvd,rlv->rkld", selector, corr, selector, precision=HIGHEST)
    lower_part, upper_part = toeplitz_tables(lag_count)
    sub_re = gathered[..., :lag_count]
    sub_im = gathered[..., lag_count:]
    gram_re = jnp.einsum("rkld,abd->rkalb", sub_re, lower_part, precision=HIGHEST) + jnp.einsum(
        "rlkd,abd->rkalb", sub_re, upper_part, precision=HIGHEST
    )
    gram_im = jnp.einsum("rkld,abd->rkalb", sub_im, lower_part, precision=HIGHEST) - jnp.einsum(
        "rlkd,abd->rkalb", sub_im, upper_part, precision=HIGHEST
    )
    gram_re = gram_re.reshape(share, taps_count, taps_count) + loading * jnp.eye(
        taps_count, dtype=jnp.float32
    )
    gram_im = gram_im.reshape(share, taps_count, taps_count)
    system = jnp.concatenate(
        [jnp.concatenate([gram_re, -gram_im], axis=2), jnp.concatenate([gram_im, gram_re], axis=2)],
        axis=1,
    )
    factor = jnp.linalg.cholesky(system)
    right_side = jnp.concatenate([cross[0], cross[1]], axis=1)
    solved = jax.vmap(
        lambda chol_factor, vector: jax.scipy.linalg.cho_solve((chol_factor, True), vector)
    )(factor, right_side)
    local_weights = jnp.stack([solved[:, :taps_count], solved[:, taps_count:]])
    weights = lax.all_gather(local_weights, "tm", axis=1, tiled=True)
    taps = weights.astype(jnp.bfloat16).reshape(2, recv_count, PER_RECV, lag_count)
    table_half = diagonal_table.astype(jnp.bfloat16)

    def second_pass(step, cancelled_all):
        start = step * batch_rows
        slots = lax.dynamic_slice_in_dim(slot, start, batch_rows, 0).reshape(-1)
        looked = jnp.take(frames, slots, axis=0).reshape(
            batch_rows, PER_RECV, 2, block_count, 2 * lag_count
        )
        tap_rows = lax.dynamic_slice_in_dim(taps, start, batch_rows, 1)
        banded = jnp.einsum(
            "vpa,xbka->xbkvp", table_half, tap_rows, preferred_element_type=jnp.float32
        ).astype(jnp.bfloat16)
        proj_re, proj_im = banded_apply(looked, banded)
        received = lax.dynamic_slice_in_dim(received_all, start, batch_rows, 1).astype(jnp.float32)
        result = jnp.stack(
            [
                received[0] - proj_re.reshape(batch_rows, length),
                received[1] - proj_im.reshape(batch_rows, length),
            ]
        ).astype(jnp.bfloat16)
        return lax.dynamic_update_slice_in_dim(cancelled_all, result, start, 1)

    cancelled = lax.fori_loop(
        0, group_count, second_pass, jnp.zeros((2, recv_count, length), jnp.bfloat16)
    )
    return (cancelled, weights)


def solution(mesh):
    in_specs = (
        P("chan", "tm"),
        P("chan", None),
        P("chan", None),
        P(None, "chan", None),
        P(None, "chan", "tm"),
    )
    out_specs = (P(None, "chan", "tm"), P(None, "chan", None))
    return jax.shard_map(local, mesh=mesh, in_specs=in_specs, out_specs=out_specs, check_vma=False)
```

profile of v0, /device:TPU:1, one launch (start us, length us, event | category | flops | bytes accessed | tf_op | source)
XLA Modules:
  0.0 828.7 jit_solution(11951167454591355933)
XLA Ops:
  14.2 6.5 collective-permute-start
  22.0 3.6 collective-permute-done
  25.7 5.1 collective-permute-start.1
  34.5 95.9 %while.45 = (s32[]{:T(128)}, f32[16,16,128]{2,0,1:T(8,128)S(1)}, bf16[16,2,128,128]{3,2,1,0:T(8,128)(2,1)S(1)}, bf16[16,2,128,64]{2,3,0,1:T(8,128)(2,1)}, s32[]{:T(128)}, /*index=5*/s32[]{:T(128)}, s32[]{}, f32[]{:T(128)}) while((s32[]{:T(128)}, f32[16,16,128]{2,0,1:T(8,128)S(1)}, bf16[16,2,128,128]{3,2,1,0:T(8,128)(2,1)S(1)}, ...), condition=%wide.region_3.4_spmd, body=%wide.region_0.3_spmd.sunk | while | flops 134610944 | bytes 14368901 | solution.py:156
  132.9 203.9 %while.47 = (s32[]{:T(128)}, bf16[2,32,8192]{2,1,0:T(8,128)(2,1)}, f32[2,32,384]{2,0,1:T(2,128)}, bf16[2,32,8192]{2,1,0:T(8,128)(2,1)}, s32[32,6]{1,0:T(8,128)S(...) while((s32[]{:T(128)}, bf16[2,32,8192]{2,1,0:T(8,128)(2,1)}, ...), condition=%wide.region_20.22_spmd.clone, body=%wide.region_17.21_spmd.clone.sunk | while | flops 1820216704 | bytes 142606928 | solution.py:204
  133.3 3.8 subtract_convert_fusion.2
  138.3 2.7 gather_fusion
  162.1 5.2 reshape.1090
  175.3 5.2 reshape.1087
  184.2 3.8 subtract_convert_fusion.2
  189.2 2.7 gather_fusion
  213.0 5.2 reshape.1090
  226.2 5.2 reshape.1087
  235.1 3.8 subtract_convert_fusion.2
  240.1 2.7 gather_fusion
  263.9 5.2 reshape.1090
  277.1 5.2 reshape.1087
  285.9 3.8 subtract_convert_fusion.2
  290.9 2.7 gather_fusion
  314.8 5.2 reshape.1090
  327.9 5.2 reshape.1087
  337.5 110.9 %all-reduce.9.cloned.1.call-done = (f32[16,16,128]{2,0,1:T(8,128)}, f32[2,32,384]{2,0,1:T(2,128)}) async-done(((f32[16,16,128]{2,0,1:T(8,128)}, f32[2,32,384]{2,0,1:T(2,128)}), (f32[16,16,128]{2,0,1:T(8,128)}, f32[2,32,384]{2,0,1:T(2,128)})) %all-reduce.9.cloned.1.call-update) | async-done | bytes 229392 | tf_op jit(solution)/shard_map/psum | solution.py:206
  449.7 3.2 fusion.67
  452.9 4.3 fusion.69
  457.2 4.2 bitcast_subtract_fusion
  464.8 5.4 bitcast_add_fusion.1
  483.8 11.7 %custom-call.56 = f32[1,128,128]{2,1,0:T(8,128)S(1)} custom-call(f32[1,128,128]{2,1,0:T(8,128)S(1)} %cholesky.427), custom_call_target="Cholesky" | custom-call | tf_op jit(solution)/shard_map/jit(cholesky)/cholesky | solution.py:230
  496.3 10.6 %custom-call.57 = f32[1,1,128,128]{2,3,1,0:T(8,128)S(1)} custom-call(f32[1,1,128,128]{3,2,1,0:T(8,128)} %get-tuple-element.625), custom_call_target="InvertDiagBlocksLowerTriangular" | custom-call | tf_op jit(solution)/shard_map/jit(cholesky)/cholesky | solution.py:230
  510.5 12.3 %custom-call.58 = f32[1,128,128]{2,1,0:T(8,128)} custom-call(f32[1,128,128]{2,1,0:T(8,128)S(1)} %cholesky.431), custom_call_target="Cholesky" | custom-call | tf_op jit(solution)/shard_map/jit(cholesky)/cholesky | solution.py:230
  525.0 10.6 %custom-call.59 = f32[1,1,128,128]{2,3,1,0:T(8,128)} custom-call(f32[1,1,128,128]{3,2,1,0:T(8,128)S(1)} %get-tuple-element.622), custom_call_target="InvertDiagBlocksLowerTriangular" | custom-call | tf_op jit(solution)/shard_map/jit(cholesky)/cholesky | solution.py:230
  539.2 12.3 %custom-call.60 = f32[1,128,128]{2,1,0:T(8,128)} custom-call(f32[1,128,128]{2,1,0:T(8,128)S(1)} %cholesky.436), custom_call_target="Cholesky" | custom-call | tf_op jit(solution)/shard_map/jit(cholesky)/cholesky | solution.py:230
  553.1 10.4 %custom-call.61 = f32[1,1,128,128]{2,3,1,0:T(8,128)} custom-call(f32[1,1,128,128]{3,2,1,0:T(8,128)S(1)} %get-tuple-element.619), custom_call_target="InvertDiagBlocksLowerTriangular" | custom-call | tf_op jit(solution)/shard_map/jit(cholesky)/cholesky | solution.py:230
  567.0 12.5 %custom-call.62 = f32[1,128,128]{2,1,0:T(8,128)} custom-call(f32[1,128,128]{2,1,0:T(8,128)S(1)} %cholesky.441), custom_call_target="Cholesky" | custom-call | tf_op jit(solution)/shard_map/jit(cholesky)/cholesky | solution.py:230
  581.1 10.4 %custom-call.63 = f32[1,1,128,128]{2,3,1,0:T(8,128)} custom-call(f32[1,1,128,128]{3,2,1,0:T(8,128)S(1)} %get-tuple-element.616), custom_call_target="InvertDiagBlocksLowerTriangular" | custom-call | tf_op jit(solution)/shard_map/jit(cholesky)/cholesky | solution.py:230
  594.9 12.3 %custom-call.64 = f32[1,128,128]{2,1,0:T(8,128)} custom-call(f32[1,128,128]{2,1,0:T(8,128)S(1)} %cholesky.446), custom_call_target="Cholesky" | custom-call | tf_op jit(solution)/shard_map/jit(cholesky)/cholesky | solution.py:230
  608.8 10.4 %custom-call.65 = f32[1,1,128,128]{2,3,1,0:T(8,128)} custom-call(f32[1,1,128,128]{3,2,1,0:T(8,128)S(1)} %get-tuple-element.613), custom_call_target="InvertDiagBlocksLowerTriangular" | custom-call | tf_op jit(solution)/shard_map/jit(cholesky)/cholesky | solution.py:230
  621.6 12.7 %custom-call.66 = f32[1,128,128]{2,1,0:T(8,128)} custom-call(f32[1,128,128]{2,1,0:T(8,128)S(1)} %fusion.93), custom_call_target="Cholesky" | custom-call | tf_op jit(solution)/shard_map/jit(cholesky)/cholesky | solution.py:230
  641.3 21.0 %while.46 = (s32[]{:T(128)}, f32[1,768,768]{2,1,0:T(8,128)}, s32[6,2]{0,1:T(2,128)S(1)}, f32[6,1,128,128]{3,2,1,0:T(8,128)}, s32[]{:T(128)}) while((s32[]{:T(128)}, f32[1,768,768]{2,1,0:T(8,128)}, s32[6,2]{0,1:T(2,128)S(1)}, f32[6,1,128,128]{3,2,1,0:T(8,128)}, s32[]{:T(128)}) %tuple.166), condition=%wide.while_cond, body=%wide.while_body.sunk | while | flops 2 | bytes 132705 | solution.py:233
  641.9 2.9 bitcast_dynamic-update-slice_fusion.2
  645.4 2.9 bitcast_dynamic-update-slice_fusion.2
  649.0 2.9 bitcast_dynamic-update-slice_fusion.2
  652.5 2.9 bitcast_dynamic-update-slice_fusion.2
  656.0 2.9 bitcast_dynamic-update-slice_fusion.2
  659.5 2.8 bitcast_dynamic-update-slice_fusion.2
  662.3 59.8 %custom-call.67 = f32[1,6,128,128]{2,3,1,0:T(8,128)S(1)} custom-call(f32[1,6,128,128]{3,2,1,0:T(8,128)} %bitcast.868), custom_call_target="InvertDiagBlocksLowerTriangular" | custom-call | tf_op jit(solution)/shard_map/vmap(jit(_cho_solve))/triangular_solve | solution.py:233
  737.8 23.6 %all_gather.3 = f32[2,32,384]{2,0,1:T(2,128)S(1)} all-gather(f32[2,1,384]{2,0,1:T(2,128)S(1)} %pad_maximum_fusion.5), channel_id=1, replica_groups=mesh['chan'=8,'tm'=32] {'tm'}, dimensions={1}, use_global_device_ids=true | all-gather | bytes 101376 | tf_op jit(solution)/shard_map/all_gather | solution.py:236
  763.9 57.8 %while.48 = (s32[]{:T(128)}, bf16[2,32,8192]{2,1,0:T(8,128)(2,1)}, bf16[2,32,8192]{2,1,0:T(8,128)(2,1)}, s32[32,6]{1,0:T(8,128)S(1)}, bf16[16,2,128,128]{3,2,1,0...) while((s32[]{:T(128)}, bf16[2,32,8192]{2,1,0:T(8,128)(2,1)}, ...), condition=%wide.region_23.25_spmd.clone, body=%wide.region_22.24_spmd.clone.sunk | while | flops 508298688 | bytes 64534532 | solution.py:260
  764.2 2.7 gather_fusion.1
  (800 shorter events, 365.5 us)
Async XLA Ops:
  7.2 441.2 %all-reduce.9.cloned.1.call-start = ((), (), s32[]{:S(2)}) async-start(), calls=%async_computation | async-start | bytes 458752 | tf_op jit(solution)/shard_map/psum | solution.py:206
  12.9 8.4 %copy-start.17 = (s32[32,6]{0,1:T(8,128)S(1)}, s32[32,6]{0,1:T(8,128)}, u32[]{:S(2)}) copy-start(s32[32,6]{0,1:T(8,128)} %param.14) | copy-start | bytes 2308
  14.2 11.4 %collective-permute-start = (bf16[8,2,8192]{2,0,1:T(8,128)(2,1)S(1)}, bf16[8,2,8192]{2,0,1:T(8,128)(2,1)S(1)}, u32[]{:S(2)}, u32[]{:S(2)}) collective-permute-start(bf16[8,2,8192]{2,0,1:T(8,128)(2,1)S(1)} %pad_maximum_fusion.2), channel_id=1, source_target_pairs={{0,224},{32,0},{64,32},{96,64},{128,96},{160,128},{192,160},{224,1... | collective-permute-start | bytes 786440 | tf_op jit(solution)/shard_map/ppermute | solution.py:17
  25.7 5.6 collective-permute-start.1
  34.5 98.4 %copy-start.15 = (f32[2,32,6]{1,0,2:T(2,128)S(1)}, f32[2,32,6]{1,0,2:T(2,128)}, u32[]{:S(2)}) copy-start(f32[2,32,6]{1,0,2:T(2,128)} %param.16) | copy-start | bytes 4612
  34.5 98.3 %copy-start.16 = (s32[32,6]{0,1:T(8,128)S(1)}, s32[32,6]{0,1:T(8,128)}, u32[]{:S(2)}) copy-start(s32[32,6]{0,1:T(8,128)} %param.15) | copy-start | bytes 2308
  132.9 204.0 %copy-start.19 = (u32[256]{0:T(256)S(1)}, u32[256]{0:T(256)}, u32[]{:S(2)}) copy-start(u32[256]{0:T(256)} %constant.562) | copy-start | bytes 3076
  132.9 316.9 %copy-start.14 = (s32[64,64]{1,0:T(8,128)S(1)}, s32[64,64]{1,0:T(8,128)}, u32[]{:S(2)}) copy-start(s32[64,64]{1,0:T(8,128)} %iota_subtract_fusion.1) | copy-start | bytes 49156
  138.2 5.5 copy-start.5
  143.7 3.0 copy-start
  143.7 1.7 copy-start.6
  147.8 2.6 copy-start.1
  169.4 2.4 copy-start.2
  189.1 5.5 copy-start.5
  194.5 3.0 copy-start
  194.6 1.7 copy-start.6
  198.7 2.6 copy-start.1
  220.3 2.4 copy-start.2
  240.0 5.5 copy-start.5
  245.4 3.0 copy-start
  245.4 1.7 copy-start.6
  249.5 2.6 copy-start.1
  271.2 2.4 copy-start.2
  290.8 5.5 copy-start.5
  296.3 3.0 copy-start
  296.3 1.7 copy-start.6
  300.4 2.6 copy-start.1
  322.1 2.4 copy-start.2
  336.8 120.4 %copy-start.18 = (pred[64]{0:T(512)(128)(4,1)S(1)}, pred[64]{0:T(512)(128)(4,1)}, u32[]{:S(2)}) copy-start(pred[64]{0:T(512)(128)(4,1)} %iota_compare_fusion.11) | copy-start | bytes 196
  463.9 10.7 %copy-start.7 = (f32[1,384,384]{1,2,0:T(8,128)}, f32[1,384,384]{1,2,0:T(8,128)S(1)}, u32[]{:S(2)}) copy-start(f32[1,384,384]{1,2,0:T(8,128)S(1)} %reshape.1060) | copy-start | bytes 1769476
  474.6 0.8 copy-start.9
  482.4 1.4 copy-start.8
  509.8 0.7 copy-start.10
  538.4 0.7 copy-start.11
  566.3 0.7 copy-start.12
  594.2 0.7 copy-start.13
  639.7 1.6 copy-start.20
  769.6 2.7 copy-start.3
  773.3 2.4 copy-start.4
  784.0 2.7 copy-start.3
  787.7 2.4 copy-start.4
  798.4 2.7 copy-start.3
  802.1 2.4 copy-start.4
  812.8 2.7 copy-start.3
  816.5 2.4 copy-start.4
Sparse Core Ops, SparseCore 0:
  336.9 111.3 all-reduce.8
where the time goes:
time: 838 us; the launch traced here: 829 us
  other arithmetic  266 us (32%)
  local copies, waits for them, and re-layouts  230 us (27%)
  matrix products  160 us (19%)
  waiting for transfers between devices  114 us (14%)
  blocking collectives  23.6 us (3%)
  between operations  18.6 us (2%)
  starting transfers between devices  11.6 us (1%)
    another operation x23, other arithmetic, local(): factor = jnp.linalg.cholesky(system)  136 us
    psum x1, waiting for transfers between devices, local(): corr = lax.psum(corr_part, 'tm')  111 us
    reshape x40, local copies, waits for them, and re-layouts, lag_sums(): flat.reshape(leading + (lag_count, width + 1))[..., 1:lag_count + 1]  81.1 us
    another operation x3, other arithmetic, local(): jax.scipy.linalg.cho_solve((chol_factor, True), vector)  61.9 us
    all_gather x1, blocking collectives, local(): weights = lax.all_gather(local_weights, 'tm', axis=1, tiled=True)  23.6 us
    another operation x21, local copies, waits for them, and re-layouts  23.2 us
    reduce_sum x40, other arithmetic, lag_sums(): return jnp.flip(jnp.sum(skewed, axis=-2), axis=-1)  22 us
    dot_general x12, matrix products, banded_apply(): jnp.einsum('bkqv,bkvp->bqp', looked[:, :, 1], banded[1], preferred_elemen...  21 us
  transfers between devices with their start and end apart: 3, of which 2 were waited for; matrix products, arithmetic and copies ran while one was open for 0% of the time, Pallas kernels for 0%

commit v1 on v0

--- a/solution.py
+++ b/solution.py
@@ -1,3 +1,4 @@
+import functools
 import math
 import jax
 import jax.numpy as jnp
@@ -10,6 +11,13 @@
 loading = 0.1
 batch_rows = 8
 HIGHEST = lax.Precision.HIGHEST
+
+
+def search_side_for(w_in, mesh_name):
+    return lax.all_gather(w_in, axis_name=mesh_name).sum(axis=0)
+
+
+group_sums_all = functools.partial(search_side_for, mesh_name="tm")
 
 
 def passed_along(array, axis, by):
@@ -203,7 +211,7 @@
     cross_init = jnp.zeros((2, recv_count, taps_count), jnp.float32)
     received_all, cross_all = lax.fori_loop(0, group_count, first_pass, (received_init, cross_init))
     share = recv_count // tm_count
-    corr = lax.psum(corr_part, "tm")
+    corr = group_sums_all(corr_part)
     cross = lax.psum_scatter(cross_all, "tm", scatter_dimension=1, tiled=True)
     mine = lax.dynamic_slice_in_dim(slot, tm_index * share, share, 0)
     selector = (

time: 838 us -> 877 us (1.047)
  waiting for transfers between devices: 114 us -> 164 us
  matrix products: 160 us -> 128 us
  local copies, waits for them, and re-layouts: 230 us -> 247 us
    psum x1 -> x0, waiting for transfers between devices: 111 us -> none  [local(): corr = lax.psum(corr_part, 'tm')]
    unnamed x1 -> x3, waiting for transfers between devices: 0.02 us -> 107 us
    all_gather x0 -> x1, waiting for transfers between devices: none -> 52.5 us  [search_side_for(): return lax.all_gather(w_in, axis_name=mesh_name).sum(axis=0)]
    dot_general x12, matrix products: 21 us -> 7.76 us  [banded_apply(): jnp.einsum('bkqv,bkvp->bqp', looked[:, :, 1], banded[1], preferred_elemen...]
  transfers between devices with their start and end apart: 3 -> 4, of which waited for: 2 -> 4; matrix products, arithmetic and copies ran while one was open for 0% -> 1% of each run, Pallas kernels for 0% -> 0%
where the time goes in v1:
time: 877 us; the launch traced here: 868 us
  other arithmetic  271 us (31%)
  local copies, waits for them, and re-layouts  247 us (28%)
  waiting for transfers between devices  164 us (19%)
  matrix products  128 us (15%)
  blocking collectives  24 us (3%)
  between operations  18.7 us (2%)
  starting transfers between devices  11.6 us (1%)
    another operation x23, other arithmetic, local(): factor = jnp.linalg.cholesky(system)  136 us
    unnamed x3, waiting for transfers between devices  107 us
    reshape x40, local copies, waits for them, and re-layouts, lag_sums(): flat.reshape(leading + (lag_count, width + 1))[..., 1:lag_count + 1]  85.5 us
    another operation x3, other arithmetic, local(): jax.scipy.linalg.cho_solve((chol_factor, True), vector)  61.4 us
    all_gather x1, waiting for transfers between devices, search_side_for(): return lax.all_gather(w_in, axis_name=mesh_name).sum(axis=0)  52.5 us
    all_gather x1, blocking collectives, local(): weights = lax.all_gather(local_weights, 'tm', axis=1, tiled=True)  24 us
    another operation x21, local copies, waits for them, and re-layouts  23.2 us
    reduce_sum x40, other arithmetic, lag_sums(): return jnp.flip(jnp.sum(skewed, axis=-2), axis=-1)  22 us
  transfers between devices with their start and end apart: 4, of which 4 were waited for; matrix products, arithmetic and copies ran while one was open for 1% of the time, Pallas kernels for 0%

profile of v1, /device:TPU:1, one launch (start us, length us, event | category | flops | bytes accessed | tf_op | source)
XLA Modules:
  0.0 868.4 jit_solution(7287134889880938872)
XLA Ops:
  14.2 6.5 collective-permute-start
  20.8 4.8 collective-permute-done
  25.7 5.0 collective-permute-start.1
  34.2 95.0 %while.45 = (s32[]{:T(128)}, f32[16,16,128]{2,1,0:T(8,128)S(1)}, bf16[16,2,128,128]{3,2,1,0:T(8,128)(2,1)S(1)}, bf16[16,2,128,64]{2,3,0,1:T(8,128)(2,1)}, s32[]{:T(128)}, /*index=5*/s32[]{:T(128)}, s32[]{}, f32[]{:T(128)}) while((s32[]{:T(128)}, f32[16,16,128]{2,1,0:T(8,128)S(1)}, bf16[16,2,128,128]{3,2,1,0:T(8,128)(2,1)S(1)}, ...), condition=%wide.region_3.4_spmd, body=%wide.region_0.3_spmd.sunk | while | flops 134610944 | bytes 14360717 | solution.py:164
  130.4 203.5 %while.47 = (s32[]{:T(128)}, bf16[2,32,8192]{2,1,0:T(8,128)(2,1)}, f32[2,32,384]{2,0,1:T(2,128)S(1)}, bf16[2,32,8192]{2,1,0:T(8,128)(2,1)}, s32[32,6]{1,0:T(8,12...) while((s32[]{:T(128)}, bf16[2,32,8192]{2,1,0:T(8,128)(2,1)}, ...), condition=%wide.region_20.22_spmd.clone, body=%wide.region_17.21_spmd.clone.sunk | while | flops 1820216704 | bytes 139732624 | solution.py:212
  132.0 3.8 subtract_convert_fusion.2
  136.9 2.8 gather_fusion
  165.6 6.3 reshape.1088
  174.0 5.2 reshape.1091
  182.8 3.8 subtract_convert_fusion.2
  187.7 2.8 gather_fusion
  216.4 6.3 reshape.1088
  224.8 5.2 reshape.1091
  233.5 3.8 subtract_convert_fusion.2
  238.5 2.8 gather_fusion
  267.2 6.3 reshape.1088
  275.6 5.2 reshape.1091
  284.3 3.8 subtract_convert_fusion.2
  317.9 6.3 reshape.1088
  326.3 5.2 reshape.1091
  337.6 106.5 %all-reduce.8.cloned.1.call-done = f32[2,32,384]{2,0,1:T(2,128)} async-done(((f32[2,32,384]{2,0,1:T(2,128)}), f32[2,32,384]{2,0,1:T(2,128)}) %all-reduce.8.cloned.1.call-update) | async-done | bytes 98320
  445.5 52.5 %all-gather.3.cloned.1.call-done = f32[512,16,128]{2,1,0:T(8,128)} async-done(((f32[16,16,128]{2,1,0:T(8,128)}), f32[512,16,128]{2,1,0:T(8,128)}) %all-gather.3.cloned.1.call-update) | async-done | bytes 4194320 | tf_op jit(solution)/shard_map/all_gather | solution.py:17
  501.0 3.2 fusion.70
  504.2 4.2 fusion.68
  508.4 4.2 bitcast_add_fusion.1
  516.0 5.4 bitcast_subtract_fusion
  525.4 2.9 maximum_maximum_fusion
  534.2 11.7 %custom-call.56 = f32[1,128,128]{2,1,0:T(8,128)S(1)} custom-call(f32[1,128,128]{2,1,0:T(8,128)S(1)} %cholesky.427), custom_call_target="Cholesky" | custom-call | tf_op jit(solution)/shard_map/jit(cholesky)/cholesky | solution.py:238
  547.4 10.6 %custom-call.57 = f32[1,1,128,128]{2,3,1,0:T(8,128)S(1)} custom-call(f32[1,1,128,128]{3,2,1,0:T(8,128)} %get-tuple-element.645), custom_call_target="InvertDiagBlocksLowerTriangular" | custom-call | tf_op jit(solution)/shard_map/jit(cholesky)/cholesky | solution.py:238
  562.2 12.5 %custom-call.58 = f32[1,128,128]{2,1,0:T(8,128)S(1)} custom-call(f32[1,128,128]{2,1,0:T(8,128)} %cholesky.431), custom_call_target="Cholesky" | custom-call | tf_op jit(solution)/shard_map/jit(cholesky)/cholesky | solution.py:238
  576.0 10.8 %custom-call.59 = f32[1,1,128,128]{2,3,1,0:T(8,128)S(1)} custom-call(f32[1,1,128,128]{3,2,1,0:T(8,128)} %get-tuple-element.642), custom_call_target="InvertDiagBlocksLowerTriangular" | custom-call | tf_op jit(solution)/shard_map/jit(cholesky)/cholesky | solution.py:238
  590.4 12.3 %custom-call.60 = f32[1,128,128]{2,1,0:T(8,128)} custom-call(f32[1,128,128]{2,1,0:T(8,128)S(1)} %cholesky.436), custom_call_target="Cholesky" | custom-call | tf_op jit(solution)/shard_map/jit(cholesky)/cholesky | solution.py:238
  604.3 10.4 %custom-call.61 = f32[1,1,128,128]{2,3,1,0:T(8,128)} custom-call(f32[1,1,128,128]{3,2,1,0:T(8,128)S(1)} %get-tuple-element.639), custom_call_target="InvertDiagBlocksLowerTriangular" | custom-call | tf_op jit(solution)/shard_map/jit(cholesky)/cholesky | solution.py:238
  618.3 12.5 %custom-call.62 = f32[1,128,128]{2,1,0:T(8,128)} custom-call(f32[1,128,128]{2,1,0:T(8,128)S(1)} %cholesky.441), custom_call_target="Cholesky" | custom-call | tf_op jit(solution)/shard_map/jit(cholesky)/cholesky | solution.py:238
  632.3 10.4 %custom-call.63 = f32[1,1,128,128]{2,3,1,0:T(8,128)} custom-call(f32[1,1,128,128]{3,2,1,0:T(8,128)S(1)} %get-tuple-element.636), custom_call_target="InvertDiagBlocksLowerTriangular" | custom-call | tf_op jit(solution)/shard_map/jit(cholesky)/cholesky | solution.py:238
  646.1 12.3 %custom-call.64 = f32[1,128,128]{2,1,0:T(8,128)} custom-call(f32[1,128,128]{2,1,0:T(8,128)S(1)} %cholesky.446), custom_call_target="Cholesky" | custom-call | tf_op jit(solution)/shard_map/jit(cholesky)/cholesky | solution.py:238
  660.0 10.4 %custom-call.65 = f32[1,1,128,128]{2,3,1,0:T(8,128)} custom-call(f32[1,1,128,128]{3,2,1,0:T(8,128)S(1)} %get-tuple-element.633), custom_call_target="InvertDiagBlocksLowerTriangular" | custom-call | tf_op jit(solution)/shard_map/jit(cholesky)/cholesky | solution.py:238
  672.8 12.7 %custom-call.66 = f32[1,128,128]{2,1,0:T(8,128)} custom-call(f32[1,128,128]{2,1,0:T(8,128)S(1)} %fusion.94), custom_call_target="Cholesky" | custom-call | tf_op jit(solution)/shard_map/jit(cholesky)/cholesky | solution.py:238
  692.5 21.0 %while.46 = (s32[]{:T(128)}, f32[1,768,768]{2,1,0:T(8,128)}, s32[6,2]{0,1:T(2,128)S(1)}, f32[6,1,128,128]{3,2,1,0:T(8,128)}, s32[]{:T(128)}) while((s32[]{:T(128)}, f32[1,768,768]{2,1,0:T(8,128)}, s32[6,2]{0,1:T(2,128)S(1)}, f32[6,1,128,128]{3,2,1,0:T(8,128)}, s32[]{:T(128)}) %tuple.170), condition=%wide.while_cond, body=%wide.while_body.sunk | while | flops 2 | bytes 132205 | solution.py:241
  693.1 2.9 bitcast_dynamic-update-slice_fusion.2
  696.6 2.9 bitcast_dynamic-update-slice_fusion.2
  700.1 2.9 bitcast_dynamic-update-slice_fusion.2
  703.7 2.9 bitcast_dynamic-update-slice_fusion.2
  707.2 2.9 bitcast_dynamic-update-slice_fusion.2
  710.7 2.8 bitcast_dynamic-update-slice_fusion.2
  713.5 59.8 %custom-call.67 = f32[1,6,128,128]{2,3,1,0:T(8,128)S(1)} custom-call(f32[1,6,128,128]{3,2,1,0:T(8,128)} %bitcast.869), custom_call_target="InvertDiagBlocksLowerTriangular" | custom-call | tf_op jit(solution)/shard_map/vmap(jit(_cho_solve))/triangular_solve | solution.py:241
  787.7 24.0 %all_gather.11 = f32[2,32,384]{2,0,1:T(2,128)S(1)} all-gather(f32[2,1,384]{2,0,1:T(2,128)S(1)} %pad_maximum_fusion.4), channel_id=1, replica_groups=mesh['chan'=8,'tm'=32] {'tm'}, dimensions={1}, use_global_device_ids=true | all-gather | bytes 101376 | tf_op jit(solution)/shard_map/all_gather | solution.py:244
  813.6 47.8 %while.48 = (s32[]{:T(128)}, bf16[2,32,8192]{2,1,0:T(8,128)(2,1)}, bf16[2,32,8192]{2,1,0:T(8,128)(2,1)}, s32[32,6]{1,0:T(8,128)S(1)}, bf16[16,2,128,128]{3,2,1,0...) while((s32[]{:T(128)}, bf16[2,32,8192]{2,1,0:T(8,128)(2,1)}, ...), condition=%wide.region_23.25_spmd.clone, body=%wide.region_22.24_spmd.clone.sunk | while | flops 508298688 | bytes 39385036 | solution.py:268
  (776 shorter events, 352.9 us)
Async XLA Ops:
  7.2 437.0 %all-reduce.8.cloned.1.call-start = ((), (), s32[]{:S(2)}) async-start(), calls=%async_computation.1 | async-start | bytes 196608
  12.9 7.8 copy-start.17
  14.2 11.5 %collective-permute-start = (bf16[8,2,8192]{2,0,1:T(8,128)(2,1)S(1)}, bf16[8,2,8192]{2,0,1:T(8,128)(2,1)S(1)}, u32[]{:S(2)}, u32[]{:S(2)}) collective-permute-start(bf16[8,2,8192]{2,0,1:T(8,128)(2,1)S(1)} %pad_maximum_fusion.1), channel_id=1, source_target_pairs={{0,224},{32,0},{64,32},{96,64},{128,96},{160,128},{192,160},{224,1... | collective-permute-start | bytes 786440 | tf_op jit(solution)/shard_map/ppermute | solution.py:25
  25.7 5.3 collective-permute-start.1
  34.2 96.2 %copy-start.12 = (f32[2,32,6]{1,0,2:T(2,128)S(1)}, f32[2,32,6]{1,0,2:T(2,128)}, u32[]{:S(2)}) copy-start(f32[2,32,6]{1,0,2:T(2,128)} %param.16) | copy-start | bytes 4612
  34.2 96.2 %copy-start.15 = (s32[32,6]{0,1:T(8,128)S(1)}, s32[32,6]{0,1:T(8,128)}, u32[]{:S(2)}) copy-start(s32[32,6]{0,1:T(8,128)} %param.15) | copy-start | bytes 2308
  129.2 1.1 copy-start.14
  142.4 5.5 copy-start
  143.0 1.6 copy-start.3
  150.9 2.9 copy-start.1
  155.8 2.4 copy-start.2
  174.0 7.3 copy-start.13
  174.0 7.3 copy-start.16
  193.1 5.5 copy-start
  193.8 1.6 copy-start.3
  201.7 2.9 copy-start.1
  206.5 2.4 copy-start.2
  224.8 7.3 copy-start.13
  224.8 7.3 copy-start.16
  243.9 5.5 copy-start
  244.6 1.6 copy-start.3
  252.4 2.9 copy-start.1
  257.3 2.4 copy-start.2
  275.6 7.3 copy-start.13
  275.6 7.3 copy-start.16
  294.7 5.5 copy-start
  295.4 1.6 copy-start.3
  303.2 2.9 copy-start.1
  308.1 2.4 copy-start.2
  326.3 7.3 copy-start.13
  326.3 7.3 copy-start.16
  333.9 0.6 copy-start.11
  334.6 163.5 %all-gather.3.cloned.1.call-start = ((), (), s32[]{:S(2)}) async-start(), calls=%async_computation | async-start | bytes 4325376 | tf_op jit(solution)/shard_map/all_gather | solution.py:17
  523.8 0.8 copy-start.4
  524.6 0.8 copy-start.6
  532.7 1.4 copy-start.5
  560.8 0.7 copy-start.7
  589.7 0.7 copy-start.8
  617.6 0.7 copy-start.9
  645.4 0.7 copy-start.10
Sparse Core Ops, SparseCore 0:
  334.7 109.3 all-reduce.7
  447.2 50.7 all-gather.2
